TPU v7x, 32 devices: a whole 2x2x4 slice. The times are simulated.
32 devices in a mesh: img: 8 (over z, y), rep: 4 (over x, core).
Axes of the slice: x: 2, y: 2, z: 4, core: 2. Of those that a mesh axis runs over, the one named last changes fastest.
Arguments:
- descriptors: bfloat16 [16, 256, 1024], P('img', 'rep'), may hold values from -0.5 to 0.5
- cell_counts: int32 [16, 256], P('img', 'rep'), may hold values from 1 to 8
- pair_images: int32 [64, 2], P('img'), may hold values from 0 to 15, as said below
- query_cells: int32 [64, 16], P('img'), may hold values from 0 to 255
- cand_cells: int32 [64, 4, 16], P('img', 'rep'), may hold values from 0 to 255, as said below
- cand_counts: int32 [64, 4], P('img', 'rep'), may hold values from 8 to 16, as said below
Outputs:
- matches: float32 [64, 2, 128], P('img')
- image_score: float32 [16], P('img')
Inputs may be any that keep to these rules, and one draw needn't show every extreme that they name: `pair_images`: the pairs are numbered by blocks of 8: pair k * 8 + j has its first image among images k * 2 to k * 2 + 1 and its second among images j * 2 to j * 2 + 1; the two images of a pair differ. cand_cells[p, r, s] lies in quarter r, between r * 64 and r * 64 + 63; cells may repeat. `cand_counts`: every count is 8 or 16, and every draw holds at least one count of 16.
All inputs are finite; a program needn't handle non-finite values.
Results may differ from a plain program's by a relative error of at most 0.0003.
Values may be sent and summed in bfloat16 or wider, within the bound.
A program may use at most 64 MiB of HBM per device.

v0:
```python
import jax
import jax.numpy as jnp
from jax import lax
from jax.sharding import PartitionSpec as P

DESC = 128
KP = 8


distant = 1000000000.0
group_size = 8


def joined(shard, axis, combine):
    everything = jax.tree.map(lambda part: lax.all_gather(part, axis), shard)
    leading = jax.tree.map(lambda part: part[0], everything)

    def turn(k, so_far):
        return combine(so_far, jax.tree.map(lambda part: part[k], everything))

    return lax.fori_loop(1, lax.axis_size(axis), turn, leading)


def nearest(queries, blocks, block_counts, live_cells):
    pairs = queries.shape[0]
    slots = blocks.shape[1]
    cands = blocks.reshape(pairs, slots * KP, DESC)
    cell_live = jnp.arange(slots, dtype=jnp.int32)[None, :] < live_cells[:, None]
    slot_live = (
        jnp.arange(KP, dtype=jnp.float32)[None, None, :]
        < block_counts.astype(jnp.float32)[:, :, None]
    )
    clive = (cell_live[:, :, None] & slot_live).reshape(pairs, slots * KP)
    groups = pairs // group_size

    def one_group(packed):
        query_part, cand_part, live_part = packed
        qwide = query_part.astype(jnp.float32)
        cwide = cand_part.astype(jnp.float32)
        qnorm = jnp.sum(qwide * qwide, axis=2)
        cnorm = jnp.sum(cwide * cwide, axis=2)
        inner = jnp.einsum(
            "pqd,pcd->pqc", query_part, cand_part, preferred_element_type=jnp.float32
        )
        dist = qnorm[:, :, None] + cnorm[:, None, :] - 2.0 * inner
        dist = jnp.where(live_part[:, None, :], dist, jnp.float32(distant))
        lowest = -lax.top_k(-dist, 2)[0]
        return (lowest[..., 0], lowest[..., 1])

    packed = (
        queries.reshape(groups, group_size, -1, DESC),
        cands.reshape(groups, group_size, -1, DESC),
        clive.reshape(groups, group_size, -1),
    )
    best, runner = lax.map(one_group, packed)
    return (best.reshape(pairs, -1), runner.reshape(pairs, -1))


def keep_two(left, right):
    low = jnp.minimum(left[0], right[0])
    high = jnp.minimum(jnp.maximum(left[0], right[0]), jnp.minimum(left[1], right[1]))
    return (low, high)


def on_device(descriptors, cell_counts, pair_images, query_cells, cand_cells, cand_counts):
    img_dev, share, width = descriptors.shape
    peers = lax.axis_size("img")
    whole, whole_counts = (
        lax.all_gather(descriptors, "rep", axis=1, tiled=True),
        lax.all_gather(cell_counts.astype(jnp.bfloat16), "rep", axis=1, tiled=True),
    )
    cells = whole.shape[1]
    first_local = pair_images[:, 0] % img_dev
    second_local = pair_images[:, 1] % img_dev
    query_rows = (first_local[:, None] * cells + query_cells).reshape(-1)
    queries = jnp.take(whole.reshape(img_dev * cells, width), query_rows, axis=0).reshape(
        peers, -1, DESC
    )
    query_counts = jnp.take(whole_counts.reshape(img_dev * cells), query_rows).reshape(peers, -1)
    qlive = (
        jnp.arange(KP, dtype=jnp.float32)[None, None, :]
        < query_counts.astype(jnp.float32)[:, :, None]
    ).reshape(peers, -1)
    lists = cand_cells[:, 0, :]
    live_cells = cand_counts[:, 0]
    local_rows = descriptors.reshape(img_dev * share, width)
    local_counts = cell_counts.reshape(img_dev * share)
    asked, asked_image = (
        lax.all_to_all(lists, "img", split_axis=0, concat_axis=0, tiled=True),
        lax.all_to_all(second_local, "img", split_axis=0, concat_axis=0, tiled=True),
    )
    rows = (asked_image[:, None] * share + asked % share).reshape(-1)
    blocks = jnp.take(local_rows, rows, axis=0).reshape(peers, -1, width)
    block_counts = jnp.take(local_counts, rows).reshape(peers, -1).astype(jnp.bfloat16)
    blocks, block_counts = (
        lax.all_to_all(blocks, "img", split_axis=0, concat_axis=0, tiled=True),
        lax.all_to_all(block_counts, "img", split_axis=0, concat_axis=0, tiled=True),
    )
    best, runner = nearest(queries, blocks, block_counts, live_cells)
    best, runner = joined((best, runner), "rep", keep_two)
    best = jnp.where(qlive, best, jnp.float32(0.0))
    runner = jnp.where(qlive, runner, jnp.float32(0.0))
    matches = jnp.stack([best, runner], axis=1)
    margin = jnp.where(qlive, (runner - best) / (runner + 1.0), jnp.float32(0.0))
    score = jnp.sum(margin, axis=1) / jnp.sum(qlive.astype(jnp.float32), axis=1)
    arrived = lax.all_to_all(score, "img", split_axis=0, concat_axis=0, tiled=True)
    image_ids = jnp.arange(img_dev, dtype=jnp.int32)
    own_part = jnp.sum(
        jnp.where(first_local[:, None] == image_ids[None, :], score[:, None], jnp.float32(0.0)),
        axis=0,
    )
    other_part = jnp.sum(
        jnp.where(asked_image[:, None] == image_ids[None, :], arrived[:, None], jnp.float32(0.0)),
        axis=0,
    )
    return (matches, own_part + other_part)


def solution(mesh):
    in_specs = (
        P("img", "rep", None),
        P("img", "rep"),
        P("img", None),
        P("img", None),
        P("img", "rep", None),
        P("img", "rep"),
    )
    out_specs = (P("img", None, None), P("img"))
    return jax.shard_map(
        on_device, mesh=mesh, in_specs=in_specs, out_specs=out_specs, check_vma=False
    )
```

profile of v0, /device:TPU:0, one launch (start us, length us, event | category | flops | bytes accessed | tf_op | source)
XLA Modules:
  0.0 107.9 jit_solution(14698842884387432103)
XLA Ops:
  7.2 0.7 all-gather.5.cloned.1.call-update
  7.9 0.7 copy.43
  8.6 7.3 %all-to-all-start = ((s32[8,1,1]{2,1,0:T(1,128)}), s32[8,1,1]{2,1,0:T(1,128)S(1)}, u32[]{:S(2)}, u32[]{:S(2)}) async-start(s32[8,1,1]{2,1,0:T(1,128)} %copy.43), calls=%async_computation | async-start | bytes 8192 | tf_op jit(solution)/shard_map/all_to_all | solution.py:90
  15.9 0.7 copy-done.3
  17.3 5.0 %all-gather.2 = bf16[4,64,2]{1,2,0:T(2,128)(2,1)S(1)} all-gather(bf16[1,64,2]{1,2,0:T(2,128)(2,1)S(1)} %convert_bitcast_fusion), channel_id=1, replica_groups=mesh['img'=8,'rep'=4] {'rep'}, dimensions={0}, use_global_device_ids=true | all-gather | bytes 1280 | tf_op jit(solution)/shard_map/all_gather | solution.py:70
  23.2 1.3 %gather_fusion = bf16[128]{0:T(256)(128)(2,1)S(1)} fusion(bf16[512]{0:T(512)(128)(2,1)S(1)} %bitcast.56, s32[1024]{0:T(1024)S(1)} %pad_clamp_fusion.1), kind=kCustom, calls=%fused_computation | custom fusion | bytes 1024 | tf_op jit(solution)/shard_map/jit(_take)/gather | solution.py:79
  24.8 6.0 %all-to-all-start.1 = ((s32[8,1,16]{2,1,0:T(1,128)}), s32[8,1,16]{2,1,0:T(1,128)S(1)}, u32[]{:S(2)}, u32[]{:S(2)}) async-start(s32[8,1,16]{2,1,0:T(1,128)} %param.12), calls=%async_computation.1 | async-start | bytes 8192 | tf_op jit(solution)/shard_map/all_to_all | solution.py:89
  31.2 6.0 %all-to-all-done.1 = s32[8,1,16]{2,1,0:T(1,128)S(1)} async-done(((s32[8,1,16]{2,1,0:T(1,128)}), s32[8,1,16]{2,1,0:T(1,128)S(1)}, u32[]{:S(2)}, u32[]{:S(2)}) %all-to-all-start.1) | async-done | bytes 544 | tf_op jit(solution)/shard_map/all_to_all | solution.py:89
  37.7 0.7 reduce.6
  38.5 1.2 %gather_fusion.1 = s32[128]{0:T(128)S(1)} fusion(s32[128]{0:T(128)S(1)} %reshape.315, s32[1024]{0:T(1024)S(1)} %pad_clamp_fusion), kind=kCustom, calls=%fused_computation.1 | custom fusion | bytes 1536 | tf_op jit(solution)/shard_map/jit(_take)/gather | solution.py:94
  40.5 3.3 %all-to-all-start.2 = ((bf16[8,1,16]{2,1,0:T(2,128)(2,1)}), bf16[8,1,16]{2,1,0:T(2,128)(2,1)S(1)}, u32[]{:S(2)}, u32[]{:S(2)}) async-start(bf16[8,1,16]{2,1,0:T(2,128)(2,1)} %copy.47), calls=%async_computation.2 | async-start | bytes 8192 | tf_op jit(solution)/shard_map/all_to_all | solution.py:97
  43.8 0.9 gather_fusion.3
  44.7 0.8 broadcast_select_fusion
  45.6 4.6 %all-to-all-done.2 = bf16[8,1,16]{2,1,0:T(2,128)(2,1)S(1)} async-done(((bf16[8,1,16]{2,1,0:T(2,128)(2,1)}), bf16[8,1,16]{2,1,0:T(2,128)(2,1)S(1)}, u32[]{:S(2)}, u32[]{:S(2)}) %all-to-all-start.2) | async-done | bytes 288 | tf_op jit(solution)/shard_map/all_to_all | solution.py:97
  50.1 3.4 %all-to-all-start.3 = ((bf16[8,16,1024]{2,1,0:T(8,128)(2,1)}), bf16[8,16,1024]{2,1,0:T(8,128)(2,1)S(1)}, u32[]{:S(2)}, u32[]{:S(2)}) async-start(bf16[8,16,1024]{2,1,0:T(8,128)(2,1)} %broadcast_select_fusion), calls=%async_computation.3 | async-start | bytes 524288 | tf_op jit(solution)/shard_map/all_to_all | solution.py:96
  54.6 7.1 %all-to-all-done.3 = bf16[8,16,1024]{2,1,0:T(8,128)(2,1)S(1)} async-done(((bf16[8,16,1024]{2,1,0:T(8,128)(2,1)}), bf16[8,16,1024]{2,1,0:T(8,128)(2,1)S(1)}, u32[]{:S(2)}, u32[]{:S(2)}) %all-to-all-start.3) | async-done | bytes 262176 | tf_op jit(solution)/shard_map/all_to_all | solution.py:96
  62.1 2.4 %gather_fusion.2 = bf16[128,1024]{1,0:T(8,128)(2,1)S(1)} fusion(bf16[512,1024]{1,0:T(8,128)(2,1)} %bitcast.58, s32[1024]{0:T(1024)S(1)} %pad_clamp_fusion.1), kind=kCustom, calls=%fused_computation.2 | custom fusion | bytes 524800 | tf_op jit(solution)/shard_map/jit(_take)/gather | solution.py:76
  64.9 2.6 %fusion.5 = f32[8,128,128]{2,1,0:T(8,128)S(1)} fusion(f32[8,128,128]{2,1,0:T(8,128)S(1)} %convolution_multiply_fusion, f32[8,128]{1,0:T(8,128)S(1)} %multiply_reduce_fusion, pred[8,128]{1,0:T(8,128)(4,1)S(1)} %compare_and_fusion.1, bf16[8,128,128]{2,1,0:T(8,128)(2,1)S(1)} %gather.29, pred[8,128]{1,0:T(8,128)(4,1)S(1)} %broadcast_in_dim.111), kind=kOutput, calls=%fused_computation.12 | output fusion | flops 918655 | bytes 1316864 | tf_op jit(solution)/shard_map/while/body/eval_jaxpr/add | solution.py:45
  67.8 10.5 %top_k.9 = (f32[8,128,128]{1,2,0:T(8,128)S(1)}, s32[8,128,128]{1,2,0:T(8,128)}) sort(f32[8,128,128]{1,2,0:T(8,128)S(1)} %copy.55, s32[8,128,128]{1,2,0:T(8,128)S(1)} %iota.21.clone), dimensions={2}, to_apply=%region_2.3 | sort | flops 2228224 | bytes 2097152 | tf_op jit(solution)/shard_map/while/body/eval_jaxpr/top_k | solution.py:47
  79.1 5.2 %all-gather = f32[32,128,1]{1,2,0:T(1,128)S(1)} all-gather(f32[8,128,1]{1,2,0:T(1,128)S(1)} %copy.49), channel_id=2, replica_groups=mesh['img'=8,'rep'=4] {'rep'}, dimensions={0}, use_global_device_ids=true | all-gather | bytes 20480 | tf_op jit(solution)/shard_map/all_gather | solution.py:15
  84.3 5.2 %all-gather.1 = f32[32,128,1]{1,2,0:T(1,128)S(1)} all-gather(f32[8,128,1]{1,2,0:T(1,128)S(1)} %copy.51), channel_id=3, replica_groups=mesh['img'=8,'rep'=4] {'rep'}, dimensions={0}, use_global_device_ids=true | all-gather | bytes 20480 | tf_op jit(solution)/shard_map/all_gather | solution.py:15
  89.8 0.7 copy.53
  90.5 3.3 %all-to-all-start.4 = ((f32[8,1,1]{2,1,0:T(1,128)}), f32[8,1,1]{2,1,0:T(1,128)S(1)}, u32[]{:S(2)}, u32[]{:S(2)}) async-start(f32[8,1,1]{2,1,0:T(1,128)} %copy.53), calls=%async_computation.4 | async-start | bytes 8192 | tf_op jit(solution)/shard_map/all_to_all | solution.py:106
  94.4 5.8 %all-to-all-done.4 = f32[8,1,1]{2,1,0:T(1,128)S(1)} async-done(((f32[8,1,1]{2,1,0:T(1,128)}), f32[8,1,1]{2,1,0:T(1,128)S(1)}, u32[]{:S(2)}, u32[]{:S(2)}) %all-to-all-start.4) | async-done | bytes 64 | tf_op jit(solution)/shard_map/all_to_all | solution.py:106
  (77 shorter events, 8.3 us)
Async XLA Ops:
  7.2 0.7 copy-start.2
  7.2 54.9 %all-gather.5.cloned.1.call-start = ((), (), s32[]{:S(2)}) async-start(), calls=%async_computation.5 | async-start | bytes 1310720 | tf_op jit(solution)/shard_map/all_gather | solution.py:69
  8.6 16.1 %all-to-all-start = ((s32[8,1,1]{2,1,0:T(1,128)}), s32[8,1,1]{2,1,0:T(1,128)S(1)}, u32[]{:S(2)}, u32[]{:S(2)}) async-start(s32[8,1,1]{2,1,0:T(1,128)} %copy.43), calls=%async_computation | async-start | bytes 8192 | tf_op jit(solution)/shard_map/all_to_all | solution.py:90
  15.9 0.7 copy-start.3
  16.6 0.7 copy-start.4
  22.4 0.7 copy-start.1
  24.8 12.4 %all-to-all-start.1 = ((s32[8,1,16]{2,1,0:T(1,128)}), s32[8,1,16]{2,1,0:T(1,128)S(1)}, u32[]{:S(2)}, u32[]{:S(2)}) async-start(s32[8,1,16]{2,1,0:T(1,128)} %param.12), calls=%async_computation.1 | async-start | bytes 8192 | tf_op jit(solution)/shard_map/all_to_all | solution.py:89
  38.5 5.3 %copy-start = (bf16[2,64,1024]{2,1,0:T(8,128)(2,1)S(1)}, bf16[2,64,1024]{2,1,0:T(8,128)(2,1)}, u32[]{:S(2)}) copy-start(bf16[2,64,1024]{2,1,0:T(8,128)(2,1)} %param.8) | copy-start | bytes 786436
  40.5 9.7 %all-to-all-start.2 = ((bf16[8,1,16]{2,1,0:T(2,128)(2,1)}), bf16[8,1,16]{2,1,0:T(2,128)(2,1)S(1)}, u32[]{:S(2)}, u32[]{:S(2)}) async-start(bf16[8,1,16]{2,1,0:T(2,128)(2,1)} %copy.47), calls=%async_computation.2 | async-start | bytes 8192 | tf_op jit(solution)/shard_map/all_to_all | solution.py:97
  50.1 11.6 %all-to-all-start.3 = ((bf16[8,16,1024]{2,1,0:T(8,128)(2,1)}), bf16[8,16,1024]{2,1,0:T(8,128)(2,1)S(1)}, u32[]{:S(2)}, u32[]{:S(2)}) async-start(bf16[8,16,1024]{2,1,0:T(8,128)(2,1)} %broadcast_select_fusion), calls=%async_computation.3 | async-start | bytes 524288 | tf_op jit(solution)/shard_map/all_to_all | solution.py:96
  90.5 9.8 %all-to-all-start.4 = ((f32[8,1,1]{2,1,0:T(1,128)}), f32[8,1,1]{2,1,0:T(1,128)S(1)}, u32[]{:S(2)}, u32[]{:S(2)}) async-start(f32[8,1,1]{2,1,0:T(1,128)} %copy.53), calls=%async_computation.4 | async-start | bytes 8192 | tf_op jit(solution)/shard_map/all_to_all | solution.py:106
Sparse Core Ops, SparseCore 0:
  9.5 19.4 all-gather.4
where the time goes:
time: 108 us
  waiting for transfers between devices  24.2 us (22%)
  starting transfers between devices  23.4 us (22%)
  other arithmetic  16.7 us (15%)
  blocking collectives  15.4 us (14%)
  between operations  14.3 us (13%)
  local copies, waits for them, and re-layouts  13.5 us (12%)
    top_k x1, other arithmetic, one_group(): lowest = -lax.top_k(-dist, 2)[0]  10.5 us
    all_gather x2, blocking collectives, joined(): everything = jax.tree.map(lambda part: lax.all_gather(part, axis), shard)  10.4 us
    all_to_all x1, starting transfers between devices, on_device(): lax.all_to_all(second_local, 'img', split_axis=0, concat_axis=0, tiled=True)  7.31 us
    all_to_all x1, waiting for transfers between devices, on_device(): lax.all_to_all(blocks, 'img', split_axis=0, concat_axis=0, tiled=True)  7.07 us
    all_to_all x1, waiting for transfers between devices, on_device(): lax.all_to_all(lists, 'img', split_axis=0, concat_axis=0, tiled=True)  6.02 us
    all_to_all x1, starting transfers between devices, on_device(): lax.all_to_all(lists, 'img', split_axis=0, concat_axis=0, tiled=True)  6.01 us
    all_to_all x1, waiting for transfers between devices, on_device(): lax.all_to_all(score, 'img', split_axis=0, concat_axis=0, tiled=True)  5.81 us
    all_gather x1, blocking collectives, on_device(): lax.all_gather(cell_counts.astype(jnp.bfloat16), 'rep', axis=1, tiled=True)  5.05 us
  transfers between devices with their start and end apart: 6, of which 4 were waited for; matrix products, arithmetic and copies ran while one was open for 9% of the time, Pallas kernels for 0%

commit v1 on v0

v1 whole, which is shorter than its diff:
```python
import functools

import jax
import jax.numpy as jnp
from jax import lax
from jax.experimental import pallas as pl
from jax.experimental.pallas import tpu as pltpu
from jax.sharding import PartitionSpec as P

DESC = 128
MESH = pl.DeviceIdType.MESH
distant = 1.0e9
far_entry = 32768.0
dead_mark = -1.0e9
f32, bf16, i32 = jnp.float32, jnp.bfloat16, jnp.int32


def partner(me, step, size):
    other, bit = 0, 1
    while bit < size:
        other = other + ((me // bit + step // bit) % 2) * bit
        bit *= 2
    return other


def repeat(first, last, body):
    if last - first <= 8:
        for t in range(first, last):
            body(t)
    else:
        lax.fori_loop(first, last, lambda t, c: (body(t), c)[1], 0)


def dot_t(a, b):
    return lax.dot_general(a, b, (((1,), (1,)), ((), ())), preferred_element_type=f32)


def split(square):
    high = square.astype(bf16)
    return high, (square - high.astype(f32)).astype(bf16)


def column(row, length):
    rows = lax.broadcasted_iota(i32, (length, length), 0)
    cols = lax.broadcasted_iota(i32, (length, length), 1)
    return jnp.sum(jnp.where(rows == cols, row, 0.0), axis=1, keepdims=True)


def merge(a, b):
    low = jnp.minimum(a[0], b[0])
    high = jnp.minimum(jnp.maximum(a[0], b[0]), jnp.minimum(a[1], b[1]))
    return low, high


def lowest_two(d):
    half = d.shape[0] // 2
    a, b = d[:half], d[half:]
    two = (jnp.minimum(a, b), jnp.maximum(a, b))
    while half > 1:
        half //= 2
        two = merge((two[0][:half], two[1][:half]), (two[0][half:], two[1][half:]))
    return two


def kernel(
    n, m,
    desc, counts, pairs, qcells, ccells, ccounts,
    matches, scores,
    whole, lists_out, lists_in, cands_out, cands_in, rhs, qnorm, part_out, own, arr,
    ag_send, ag_recv, fw_send, fw_recv, list_send, list_recv, cand_send, cand_recv,
    own_send, own_recv, arr_send, arr_recv,
):
    me, r = lax.axis_index("img"), lax.axis_index("rep")
    img_dev, share, width = desc.shape
    rows = img_dev * share
    kp = width // DESC
    slots = ccells.shape[2]
    qn = qcells.shape[1]
    mate, across = partner(r, 1, m), partner(r, 2, m)

    def remote(src, dst, send, recv, img, rep):
        return pltpu.make_async_remote_copy(
            src_ref=src, dst_ref=dst, send_sem=send, recv_sem=recv,
            device_id=(img, rep), device_id_type=MESH,
        )

    barrier = pltpu.get_barrier_semaphore()

    def greet_all(t):
        other = (me * m + r + t) % (n * m)
        pl.semaphore_signal(barrier, inc=1, device_id=(other // m, other % m), device_id_type=MESH)

    lax.fori_loop(1, n * m, lambda t, c: (greet_all(t), c)[1], 0)

    slot_of = lax.broadcasted_iota(i32, (share, width), 1) // DESC
    for i in range(img_dev):
        live = column(counts[i : i + 1, :].astype(f32), share)
        marked = jnp.where(slot_of.astype(f32) < live, desc[i].astype(f32), far_entry)
        whole[r, i * share : (i + 1) * share, :] = marked.astype(bf16)

    second = pairs[:, 1:2] % img_dev
    wanted = second * share + ccells[:, 0, :] % share
    wanted = jnp.where(lax.broadcasted_iota(i32, (n, slots), 1) < ccounts[...], wanted, -1)
    wanted = wanted.astype(f32)
    for j in range(n):
        spread = jnp.broadcast_to(column(wanted[j : j + 1, :], slots), (slots, rows))
        lists_out[j] = spread.astype(i32)
    lists_in[me] = lists_out[me]

    pl.semaphore_wait(barrier, n * m - 1)

    def send_list(t):
        k = partner(me, t, n)
        remote(lists_out.at[k], lists_in.at[me], list_send, list_recv.at[me], k, r).start()

    repeat(1, n, send_list)

    def shard(owner, i):
        return whole.at[owner, pl.ds(i * share, share)]

    for i in range(img_dev):
        remote(shard(r, i), shard(r, i), ag_send, ag_recv.at[0, i], me, across).start()
    for i in range(img_dev):
        remote(shard(r, i), shard(r, i), ag_send, ag_recv.at[1, i], me, mate).start()

    group = n // 2
    lane = lax.broadcasted_iota(i32, (slots, rows), 1)
    for g in range(0, n, group):
        picks = []
        for t in range(g, g + group):
            k = partner(me, t, n)
            if t > 0:
                pltpu.make_async_copy(lists_out.at[k], lists_in.at[k], list_recv.at[k]).wait()
            picks.append(lists_in[k])
        asked = jnp.concatenate(picks, axis=0)
        lanes = lax.broadcasted_iota(i32, asked.shape, 1)
        chosen = (asked == lanes).astype(f32).astype(bf16)
        block = jnp.dot(chosen, whole[r], preferred_element_type=f32)
        block = jnp.where(asked[:, :1] < 0, far_entry, block).astype(bf16)
        for t in range(g, g + group):
            k = partner(me, t, n)
            part = block[(t - g) * slots : (t - g + 1) * slots]
            if t == 0:
                cands_in[me] = part
            else:
                cands_out[k] = part
        for t in range(max(g, 1), g + group):
            k = partner(me, t, n)
            remote(cands_out.at[k], cands_in.at[me], cand_send, cand_recv.at[me], k, r).start()

    for i in range(img_dev):
        pltpu.make_async_copy(shard(across, i), shard(across, i), ag_recv.at[0, i]).wait()
        remote(shard(across, i), shard(across, i), fw_send, fw_recv.at[i], me, mate).start()
    diagonal = partner(r, 3, m)
    for i in range(img_dev):
        pltpu.make_async_copy(shard(mate, i), shard(mate, i), ag_recv.at[1, i]).wait()
    for i in range(img_dev):
        pltpu.make_async_copy(shard(diagonal, i), shard(diagonal, i), fw_recv.at[i]).wait()

    first = pairs[:, 0:1] % img_dev
    cells = qcells[...]
    where = (cells // share) * rows + first * share + cells % share
    where = where.astype(f32)
    all_rows = m * rows
    picks = [
        jnp.broadcast_to(column(where[j : j + 1, :], qn), (qn, all_rows)) for j in range(n)
    ]
    asked = jnp.concatenate(picks, axis=0).astype(i32)
    chosen = (asked == lax.broadcasted_iota(i32, asked.shape, 1)).astype(f32).astype(bf16)
    found = jnp.dot(chosen, whole[...].reshape(all_rows, width), preferred_element_type=f32)
    found = found.astype(bf16)
    qd = qn * kp
    to = lax.broadcasted_iota(i32, (qd, qd), 0)
    at = lax.broadcasted_iota(i32, (qd, qd), 1)
    order = (at == (to % kp) * qn + to // kp).astype(f32).astype(bf16)
    ones = jnp.ones((qd, DESC), bf16)
    for j in range(n):
        mine = found[j * qn : (j + 1) * qn]
        stack = jnp.concatenate([mine[:, s * DESC : (s + 1) * DESC] for s in range(kp)], axis=0)
        query = jnp.dot(order, stack, preferred_element_type=f32)
        high, low = split(query * query)
        qnorm[j] = dot_t(jnp.ones((8, 2 * DESC), bf16), jnp.concatenate([high, low], axis=1))
        rhs[j] = jnp.concatenate([ones, ones, query.astype(bf16)], axis=1)

    def one_pair(t):
        j = partner(me, t, n)
        if not (isinstance(t, int) and t == 0):
            pltpu.make_async_copy(cands_out.at[j], cands_in.at[j], cand_recv.at[j]).wait()
        mine = cands_in[j]
        stack = jnp.concatenate([mine[:, s * DESC : (s + 1) * DESC] for s in range(kp)], axis=0)
        wide = stack.astype(f32)
        high, low = split(wide * wide)
        lhs = jnp.concatenate([high, low, (-2.0 * wide).astype(bf16)], axis=1)
        norm = qnorm[j][0:1]
        dist = jnp.minimum(dot_t(lhs, rhs[j]) + norm, distant)
        best, runner = lowest_two(dist)
        live = norm < distant
        two = jnp.concatenate(
            [jnp.where(live, best, dead_mark), jnp.where(live, runner, dead_mark)], axis=0
        )
        part_out[j] = two
        own[r, j] = two
        for d in range(1, m):
            to_rep = partner(r, d, m)
            remote(part_out.at[j], own.at[r, j], own_send, own_recv.at[r], me, to_rep).start()
        if not (isinstance(t, int) and t == 0):
            for d in range(m):
                to_rep = partner(r, d, m)
                remote(part_out.at[j], arr.at[r, me], arr_send, arr_recv.at[r], j, to_rep).start()

    one_pair(0)
    repeat(1, n, one_pair)

    for d in range(1, m):
        o = partner(r, d, m)
        pltpu.make_async_copy(own.at[o], own.at[o], own_recv.at[o]).wait()

    def gathered(buf):
        two = (buf[0, :, 0, :], buf[0, :, 1, :])
        for o in range(1, m):
            two = merge(two, (buf[o, :, 0, :], buf[o, :, 1, :]))
        return two

    def score_of(two):
        live = two[0] > 0.5 * dead_mark
        best, runner = jnp.where(live, two[0], 0.0), jnp.where(live, two[1], 0.0)
        margin = jnp.where(live, (runner - best) / (runner + 1.0), 0.0)
        total = jnp.sum(margin, axis=1, keepdims=True)
        return best, runner, total / jnp.sum(live.astype(f32), axis=1, keepdims=True)

    best, runner, score = score_of(gathered(own))
    matches[:, 0, :] = best
    matches[:, 1, :] = runner

    for o in range(m):
        arr[o, me] = own[o, me]
    for o in range(m):
        rest = arr.at[o, pl.ds(0, n - 1)]
        pltpu.make_async_copy(rest, rest, arr_recv.at[o]).wait()
    _, _, other_score = score_of(gathered(arr))
    asked_image = lists_in[:, 0, :][:, 0:1] // share
    for i in range(img_dev):
        scores[i] = jnp.sum(jnp.where(first == i, score, 0.0)) + jnp.sum(
            jnp.where(asked_image == i, other_score, 0.0)
        )

    def drain(ref, sem):
        pltpu.make_async_copy(ref, ref, sem).wait()

    drain(whole.at[pl.ds(0, 2)], ag_send)
    drain(whole.at[0], fw_send)
    drain(lists_out.at[pl.ds(0, n - 1)], list_send)
    drain(cands_out.at[pl.ds(0, n - 1)], cand_send)
    drain(own.at[pl.ds(0, m - 1)], own_send)
    drain(arr.at[:, pl.ds(0, n - 1)], arr_send)


def on_device(n, m, descriptors, cell_counts, pair_images, query_cells, cand_cells, cand_counts):
    img_dev, share, width = descriptors.shape
    rows, slots, qd = img_dev * share, cand_cells.shape[2], query_cells.shape[1] * width // DESC
    vmem = pl.BlockSpec(memory_space=pltpu.VMEM)
    dma = pltpu.SemaphoreType.DMA
    return pl.pallas_call(
        functools.partial(kernel, n, m),
        out_shape=(
            jax.ShapeDtypeStruct((n, 2, qd), f32),
            jax.ShapeDtypeStruct((img_dev,), f32),
        ),
        in_specs=[vmem] * 6,
        out_specs=(vmem, pl.BlockSpec(memory_space=pltpu.SMEM)),
        scratch_shapes=[
            pltpu.VMEM((m, rows, width), bf16),
            pltpu.VMEM((n, slots, rows), i32),
            pltpu.VMEM((n, slots, rows), i32),
            pltpu.VMEM((n, slots, width), bf16),
            pltpu.VMEM((n, slots, width), bf16),
            pltpu.VMEM((n, qd, 3 * DESC), bf16),
            pltpu.VMEM((n, 8, qd), f32),
            pltpu.VMEM((n, 2, qd), f32),
            pltpu.VMEM((m, n, 2, qd), f32),
            pltpu.VMEM((m, n, 2, qd), f32),
            dma, dma((2, img_dev)), dma, dma((img_dev,)),
            dma, dma((n,)), dma, dma((n,)),
            dma, dma((m,)), dma, dma((m,)),
        ],
        compiler_params=pltpu.CompilerParams(collective_id=0, has_side_effects=True),
    )(descriptors, cell_counts, pair_images, query_cells, cand_cells, cand_counts)


def solution(mesh):
    n, m = mesh.shape["img"], mesh.shape["rep"]
    in_specs = (
        P("img", "rep", None),
        P("img", "rep"),
        P("img", None),
        P("img", None),
        P("img", "rep", None),
        P("img", "rep"),
    )
    out_specs = (P("img", None, None), P("img"))
    return jax.shard_map(
        functools.partial(on_device, n, m),
        mesh=mesh, in_specs=in_specs, out_specs=out_specs, check_vma=False,
    )
```

time: 108 us -> 28.6 us (0.26)
  waiting for transfers between devices: 24.2 us -> 0 us
  Pallas kernels: 0 us -> 23.9 us
  starting transfers between devices: 23.4 us -> 0 us
  other arithmetic: 16.7 us -> 0 us
  blocking collectives: 15.4 us -> 0 us
  between operations: 14.3 us -> 0.66 us
  local copies, waits for them, and re-layouts: 13.5 us -> 3.84 us
    pallas_call x0 -> x1, Pallas kernels: none -> 23.9 us  [on_device(): pl.pallas_call(functools.partial(kernel, n, m), out_shape=(jax.ShapeDtype...]
    all_to_all x5 -> x0, waiting for transfers between devices: 23.5 us -> none  [the longest x1 7.07 us: on_device(): lax.all_to_all(blocks, 'img', split_axis=0, concat_axis=0, tiled=True)]
    all_to_all x5 -> x0, starting transfers between devices: 23.4 us -> none  [the longest x1 7.31 us: on_device(): lax.all_to_all(second_local, 'img', split_axis=0, concat_axis=0, tiled=True)]
    all_gather x3 -> x0, blocking collectives: 15.4 us -> none  [the longest x2 10.4 us: joined(): everything = jax.tree.map(lambda part: lax.all_gather(part, axis), shard)]
    top_k x1 -> x0, other arithmetic: 10.5 us -> none  [one_group(): lowest = -lax.top_k(-dist, 2)[0]]
    gather x7 -> x0, local copies, waits for them, and re-layouts: 6.03 us -> none  [the longest x2 2.52 us: on_device(): jnp.take(whole.reshape(img_dev * cells, width), query_rows, axis=0)]
    add x4 -> x0, other arithmetic: 3.2 us -> none  [the longest x1 2.6 us: one_group(): dist = qnorm[:, :, None] + cnorm[:, None, :] - 2.0 * inner]
    unnamed x14 -> x8, local copies, waits for them, and re-layouts: 2.81 us -> 3.84 us
  transfers between devices with their start and end apart: 6 -> 0, of which waited for: 4 -> 0; matrix products, arithmetic and copies ran while one was open for 9% -> 0% of each run, Pallas kernels for 0% -> 0%
where the time goes in v1:
time: 28.6 us; the launch traced here: 28.4 us
  Pallas kernels  23.9 us (84%)
  local copies, waits for them, and re-layouts  3.84 us (13%)
  between operations  0.66 us (2%)
    pallas_call x1, Pallas kernels, on_device(): pl.pallas_call(functools.partial(kernel, n, m), out_shape=(jax.ShapeDtype...  23.9 us
    unnamed x8, local copies, waits for them, and re-layouts  3.84 us

profile of v1, /device:TPU:0, one launch (start us, length us, event | category | flops | bytes accessed | tf_op | source)
XLA Modules:
  0.0 28.4 jit_solution(9238783910505955647)
XLA Ops:
  0.6 0.0 copy-start
  0.6 1.4 %copy.8.pairs = s32[8,2]{1,0:T(8,128)} copy(s32[8,2]{0,1:T(2,128)} %param.8) | data formatting | bytes 128 | tf_op args[2]
  2.0 0.0 copy-done
  2.0 0.7 %copy.9.ccounts = s32[8,1]{1,0:T(8,128)} copy(s32[8,1]{0,1:T(1,128)S(1)} %copy-done) | data formatting | bytes 64 | tf_op args[5]
  2.7 23.9 %shard_map.77 = (f32[8,2,128]{2,1,0:T(2,128)}, f32[2]{0:T(128)}) custom-call(bf16[2,64,1024]{2,1,0:T(8,128)(2,1)} %desc.1, s32[2,64]{1,0:T(2,128)} %counts.1, s32[8,2]{1,0:T(8,128)} %copy.8.pairs, s32[8,16]{1,0:T(8,128)} %qcells.1, s32[8,1,16]{2,1,0:T(1,128)} %ccells.1, s32[8,1]{1,0:T(8,128)} %copy.9.ccounts), custom_call_target="tpu_custom_call" | custom-call | tf_op jit(solution)/shard_map/pallas_call | solution.py:263
  26.6 0.0 copy-start.1
  26.6 1.3 %copy.12 = f32[8,2,128]{2,1,0:T(2,128)} copy(f32[8,2,128]{2,1,0:T(2,128)} %get-tuple-element.4) | data formatting | bytes 16384
  27.9 0.0 copy-done.1
  27.9 0.5 %copy.13 = f32[2]{0:T(128)} copy(f32[2]{0:T(128)S(1)} %copy-done.1) | data formatting | bytes 16
Async XLA Ops:
  0.6 1.4 %copy-start = (s32[8,1]{0,1:T(1,128)S(1)}, s32[8,1]{0,1:T(1,128)}, u32[]{:S(2)}) copy-start(s32[8,1]{0,1:T(1,128)} %param.11) | copy-start | bytes 100
  26.6 1.3 %copy-start.1 = (f32[2]{0:T(128)S(1)}, f32[2]{0:T(128)}, u32[]{:S(2)}) copy-start(f32[2]{0:T(128)} %get-tuple-element.5) | copy-start | bytes 28

commit v2 on v1

--- a/solution.py
+++ b/solution.py
@@ -64,8 +64,9 @@
 
 def kernel(
     n, m,
-    desc, counts, pairs, qcells, ccells, ccounts,
+    desc_hbm, counts_hbm, pairs_hbm, qcells_hbm, ccells_hbm, ccounts_hbm,
     matches, scores,
+    desc, counts, pairs, qcells, ccells, ccounts, in_sem,
     whole, lists_out, lists_in, cands_out, cands_in, rhs, qnorm, part_out, own, arr,
     ag_send, ag_recv, fw_send, fw_recv, list_send, list_recv, cand_send, cand_recv,
     own_send, own_recv, arr_send, arr_recv,
@@ -92,15 +93,30 @@
 
     lax.fori_loop(1, n * m, lambda t, c: (greet_all(t), c)[1], 0)
 
+    loads = [
+        pltpu.make_async_copy(src, dst, in_sem.at[i])
+        for i, (src, dst) in enumerate((
+            (counts_hbm, counts), (desc_hbm, desc), (pairs_hbm, pairs),
+            (ccells_hbm, ccells), (ccounts_hbm, ccounts), (qcells_hbm, qcells),
+        ))
+    ]
+    for load in loads:
+        load.start()
+    for load in loads:
+        load.wait()
+
     slot_of = lax.broadcasted_iota(i32, (share, width), 1) // DESC
     for i in range(img_dev):
         live = column(counts[i : i + 1, :].astype(f32), share)
         marked = jnp.where(slot_of.astype(f32) < live, desc[i].astype(f32), far_entry)
         whole[r, i * share : (i + 1) * share, :] = marked.astype(bf16)
 
-    second = pairs[:, 1:2] % img_dev
+    local = (pairs[...] % img_dev).astype(f32)
+    first = column(local[0:1], n).astype(i32)
+    second = column(local[1:2], n).astype(i32)
+    live_cells = column(ccounts[...].astype(f32), n).astype(i32)
     wanted = second * share + ccells[:, 0, :] % share
-    wanted = jnp.where(lax.broadcasted_iota(i32, (n, slots), 1) < ccounts[...], wanted, -1)
+    wanted = jnp.where(lax.broadcasted_iota(i32, (n, slots), 1) < live_cells, wanted, -1)
     wanted = wanted.astype(f32)
     for j in range(n):
         spread = jnp.broadcast_to(column(wanted[j : j + 1, :], slots), (slots, rows))
@@ -157,7 +173,6 @@
     for i in range(img_dev):
         pltpu.make_async_copy(shard(diagonal, i), shard(diagonal, i), fw_recv.at[i]).wait()
 
-    first = pairs[:, 0:1] % img_dev
     cells = qcells[...]
     where = (cells // share) * rows + first * share + cells % share
     where = where.astype(f32)
@@ -260,15 +275,20 @@
     rows, slots, qd = img_dev * share, cand_cells.shape[2], query_cells.shape[1] * width // DESC
     vmem = pl.BlockSpec(memory_space=pltpu.VMEM)
     dma = pltpu.SemaphoreType.DMA
+    operands = (
+        descriptors, cell_counts, pair_images.T, query_cells, cand_cells, cand_counts.T,
+    )
     return pl.pallas_call(
         functools.partial(kernel, n, m),
         out_shape=(
             jax.ShapeDtypeStruct((n, 2, qd), f32),
             jax.ShapeDtypeStruct((img_dev,), f32),
         ),
-        in_specs=[vmem] * 6,
+        in_specs=[pl.BlockSpec(memory_space=pltpu.HBM)] * 6,
         out_specs=(vmem, pl.BlockSpec(memory_space=pltpu.SMEM)),
         scratch_shapes=[
+            *(pltpu.VMEM(x.shape, x.dtype) for x in operands),
+            dma((len(operands),)),
             pltpu.VMEM((m, rows, width), bf16),
             pltpu.VMEM((n, slots, rows), i32),
             pltpu.VMEM((n, slots, rows), i32),
@@ -283,8 +303,10 @@
             dma, dma((n,)), dma, dma((n,)),
             dma, dma((m,)), dma, dma((m,)),
         ],
-        compiler_params=pltpu.CompilerParams(collective_id=0, has_side_effects=True),
-    )(descriptors, cell_counts, pair_images, query_cells, cand_cells, cand_counts)
+        compiler_params=pltpu.CompilerParams(
+            collective_id=0, has_side_effects=True
+        ),
+    )(*operands)
 
 
 def solution(mesh):

time: 28.6 us -> 25.8 us (0.902)
  local copies, waits for them, and re-layouts: 3.84 us -> 1.81 us
  Pallas kernels: 23.9 us -> 23.1 us
    unnamed x8 -> x4, local copies, waits for them, and re-layouts: 3.84 us -> 1.81 us
    pallas_call x1, Pallas kernels: 23.9 us -> 23.1 us  [on_device(): pl.pallas_call(functools.partial(kernel, n, m), out_shape=(jax.ShapeDtype...]
where the time goes in v2:
time: 25.8 us; the launch traced here: 25.6 us
  Pallas kernels  23.1 us (90%)
  local copies, waits for them, and re-layouts  1.81 us (7%)
  between operations  0.65 us (3%)
    pallas_call x1, Pallas kernels, on_device(): pl.pallas_call(functools.partial(kernel, n, m), out_shape=(jax.ShapeDtype...  23.1 us
    unnamed x4, local copies, waits for them, and re-layouts  1.81 us

profile of v2, /device:TPU:0, one launch (start us, length us, event | category | flops | bytes accessed | tf_op | source)
XLA Modules:
  0.0 25.6 jit_solution(9403867370684615972)
XLA Ops:
  0.6 23.1 %shard_map.77 = (f32[8,2,128]{2,1,0:T(2,128)}, f32[2]{0:T(128)}) custom-call(bf16[2,64,1024]{2,1,0:T(8,128)(2,1)} %desc_hbm.1, s32[2,64]{1,0:T(2,128)} %counts_hbm.1, s32[2,8]{1,0:T(2,128)} %bitcast.2, s32[8,16]{1,0:T(8,128)} %qcells_hbm.1, s32[8,1,16]{2,1,0:T(1,128)} %ccells_hbm.1, s32[1,8]{1,0:T(1,128)} %bitcast.3), custom_call_target="tpu_custom_call" | custom-call | tf_op jit(solution)/shard_map/pallas_call | solution.py:281
  23.8 0.0 copy-start
  23.8 1.3 %copy.10 = f32[8,2,128]{2,1,0:T(2,128)} copy(f32[8,2,128]{2,1,0:T(2,128)} %get-tuple-element.4) | data formatting | bytes 16384
  25.1 0.0 copy-done
  25.1 0.5 %copy.11 = f32[2]{0:T(128)} copy(f32[2]{0:T(128)S(1)} %copy-done) | data formatting | bytes 16
Async XLA Ops:
  23.8 1.3 %copy-start = (f32[2]{0:T(128)S(1)}, f32[2]{0:T(128)}, u32[]{:S(2)}) copy-start(f32[2]{0:T(128)} %get-tuple-element.5) | copy-start | bytes 28

commit v3 on v2

--- a/solution.py
+++ b/solution.py
@@ -87,11 +87,11 @@
 
     barrier = pltpu.get_barrier_semaphore()
 
-    def greet_all(t):
-        other = (me * m + r + t) % (n * m)
-        pl.semaphore_signal(barrier, inc=1, device_id=(other // m, other % m), device_id_type=MESH)
-
-    lax.fori_loop(1, n * m, lambda t, c: (greet_all(t), c)[1], 0)
+    def greet(img, rep):
+        pl.semaphore_signal(barrier, inc=1, device_id=(img, rep), device_id_type=MESH)
+
+    repeat(1, n, lambda t: greet(partner(me, t, n), r))
+    repeat(1, m, lambda t: greet(me, partner(r, t, m)))
 
     loads = [
         pltpu.make_async_copy(src, dst, in_sem.at[i])
@@ -117,13 +117,12 @@
     live_cells = column(ccounts[...].astype(f32), n).astype(i32)
     wanted = second * share + ccells[:, 0, :] % share
     wanted = jnp.where(lax.broadcasted_iota(i32, (n, slots), 1) < live_cells, wanted, -1)
-    wanted = wanted.astype(f32)
+    wanted = jnp.concatenate([wanted, jnp.zeros((n, DESC - slots), i32)], axis=1)
     for j in range(n):
-        spread = jnp.broadcast_to(column(wanted[j : j + 1, :], slots), (slots, rows))
-        lists_out[j] = spread.astype(i32)
+        lists_out[j] = wanted[j : j + 1]
     lists_in[me] = lists_out[me]
 
-    pl.semaphore_wait(barrier, n * m - 1)
+    pl.semaphore_wait(barrier, n + m - 2)
 
     def send_list(t):
         k = partner(me, t, n)
@@ -140,19 +139,18 @@
         remote(shard(r, i), shard(r, i), ag_send, ag_recv.at[1, i], me, mate).start()
 
     group = n // 2
-    lane = lax.broadcasted_iota(i32, (slots, rows), 1)
     for g in range(0, n, group):
         picks = []
         for t in range(g, g + group):
             k = partner(me, t, n)
             if t > 0:
                 pltpu.make_async_copy(lists_out.at[k], lists_in.at[k], list_recv.at[k]).wait()
-            picks.append(lists_in[k])
-        asked = jnp.concatenate(picks, axis=0)
-        lanes = lax.broadcasted_iota(i32, asked.shape, 1)
+            picks.append(column(lists_in[k][:, :slots].astype(f32), slots))
+        asked = jnp.concatenate(picks, axis=0).astype(i32)
+        lanes = lax.broadcasted_iota(i32, (group * slots, rows), 1)
         chosen = (asked == lanes).astype(f32).astype(bf16)
         block = jnp.dot(chosen, whole[r], preferred_element_type=f32)
-        block = jnp.where(asked[:, :1] < 0, far_entry, block).astype(bf16)
+        block = jnp.where(asked < 0, far_entry, block).astype(bf16)
         for t in range(g, g + group):
             k = partner(me, t, n)
             part = block[(t - g) * slots : (t - g + 1) * slots]
@@ -290,8 +288,8 @@
             *(pltpu.VMEM(x.shape, x.dtype) for x in operands),
             dma((len(operands),)),
             pltpu.VMEM((m, rows, width), bf16),
-            pltpu.VMEM((n, slots, rows), i32),
-            pltpu.VMEM((n, slots, rows), i32),
+            pltpu.VMEM((n, 1, DESC), i32),
+            pltpu.VMEM((n, 1, DESC), i32),
             pltpu.VMEM((n, slots, width), bf16),
             pltpu.VMEM((n, slots, width), bf16),
             pltpu.VMEM((n, qd, 3 * DESC), bf16),

time: 25.8 us -> 25.3 us (0.981)
  Pallas kernels: 23.1 us -> 22.6 us
    pallas_call x1, Pallas kernels: 23.1 us -> 22.6 us  [on_device(): pl.pallas_call(functools.partial(kernel, n, m), out_shape=(jax.ShapeDtype...]
where the time goes in v3:
time: 25.3 us; the launch traced here: 25.1 us
  Pallas kernels  22.6 us (89%)
  local copies, waits for them, and re-layouts  1.81 us (7%)
  between operations  0.65 us (3%)
    pallas_call x1, Pallas kernels, on_device(): pl.pallas_call(functools.partial(kernel, n, m), out_shape=(jax.ShapeDtype...  22.6 us
    unnamed x4, local copies, waits for them, and re-layouts  1.81 us

profile of v3, /device:TPU:0, one launch (start us, length us, event | category | flops | bytes accessed | tf_op | source)
XLA Modules:
  0.0 25.1 jit_solution(3722860264283497097)
XLA Ops:
  0.6 22.6 %shard_map.77 = (f32[8,2,128]{2,1,0:T(2,128)}, f32[2]{0:T(128)}) custom-call(bf16[2,64,1024]{2,1,0:T(8,128)(2,1)} %desc_hbm.1, s32[2,64]{1,0:T(2,128)} %counts_hbm.1, s32[2,8]{1,0:T(2,128)} %bitcast.2, s32[8,16]{1,0:T(8,128)} %qcells_hbm.1, s32[8,1,16]{2,1,0:T(1,128)} %ccells_hbm.1, s32[1,8]{1,0:T(1,128)} %bitcast.3), custom_call_target="tpu_custom_call" | custom-call | tf_op jit(solution)/shard_map/pallas_call | solution.py:279
  23.3 0.0 copy-start
  23.3 1.3 %copy.10 = f32[8,2,128]{2,1,0:T(2,128)} copy(f32[8,2,128]{2,1,0:T(2,128)} %get-tuple-element.4) | data formatting | bytes 16384
  24.6 0.0 copy-done
  24.6 0.5 %copy.11 = f32[2]{0:T(128)} copy(f32[2]{0:T(128)S(1)} %copy-done) | data formatting | bytes 16
Async XLA Ops:
  23.3 1.3 %copy-start = (f32[2]{0:T(128)S(1)}, f32[2]{0:T(128)}, u32[]{:S(2)}) copy-start(f32[2]{0:T(128)} %get-tuple-element.5) | copy-start | bytes 28

commit v4 on v3

--- a/solution.py
+++ b/solution.py
@@ -65,9 +65,9 @@
 def kernel(
     n, m,
     desc_hbm, counts_hbm, pairs_hbm, qcells_hbm, ccells_hbm, ccounts_hbm,
-    matches, scores,
+    own, arr, lists_hbm,
     desc, counts, pairs, qcells, ccells, ccounts, in_sem,
-    whole, lists_out, lists_in, cands_out, cands_in, rhs, qnorm, part_out, own, arr,
+    whole, lists_out, lists_in, cands_out, cands_in, rhs, qnorm, part_out, out_sem,
     ag_send, ag_recv, fw_send, fw_recv, list_send, list_recv, cand_send, cand_recv,
     own_send, own_recv, arr_send, arr_recv,
 ):
@@ -162,6 +162,9 @@
             k = partner(me, t, n)
             remote(cands_out.at[k], cands_in.at[me], cand_send, cand_recv.at[me], k, r).start()
 
+    listed = pltpu.make_async_copy(lists_in, lists_hbm, out_sem.at[0])
+    listed.start()
+
     for i in range(img_dev):
         pltpu.make_async_copy(shard(across, i), shard(across, i), ag_recv.at[0, i]).wait()
         remote(shard(across, i), shard(across, i), fw_send, fw_recv.at[i], me, mate).start()
@@ -212,7 +215,6 @@
             [jnp.where(live, best, dead_mark), jnp.where(live, runner, dead_mark)], axis=0
         )
         part_out[j] = two
-        own[r, j] = two
         for d in range(1, m):
             to_rep = partner(r, d, m)
             remote(part_out.at[j], own.at[r, j], own_send, own_recv.at[r], me, to_rep).start()
@@ -224,9 +226,30 @@
     one_pair(0)
     repeat(1, n, one_pair)
 
+    mine = pltpu.make_async_copy(part_out, own.at[r], out_sem.at[1])
+    mine.start()
+    listed.wait()
+    mine.wait()
     for d in range(1, m):
         o = partner(r, d, m)
         pltpu.make_async_copy(own.at[o], own.at[o], own_recv.at[o]).wait()
+    for o in range(m):
+        rest = arr.at[o, pl.ds(0, n - 1)]
+        pltpu.make_async_copy(rest, rest, arr_recv.at[o]).wait()
+
+    def drain(ref, sem):
+        pltpu.make_async_copy(ref, ref, sem).wait()
+
+    drain(whole.at[pl.ds(0, 2)], ag_send)
+    drain(whole.at[0], fw_send)
+    drain(lists_out.at[pl.ds(0, n - 1)], list_send)
+    drain(cands_out.at[pl.ds(0, n - 1)], cand_send)
+    drain(own.at[pl.ds(0, m - 1)], own_send)
+    drain(arr.at[:, pl.ds(0, n - 1)], arr_send)
+
+
+def finish(n, m, img_dev, share, own, arr, lists, pairs, matches, scores):
+    me = lax.axis_index("img")
 
     def gathered(buf):
         two = (buf[0, :, 0, :], buf[0, :, 1, :])
@@ -244,28 +267,14 @@
     best, runner, score = score_of(gathered(own))
     matches[:, 0, :] = best
     matches[:, 1, :] = runner
-
-    for o in range(m):
-        arr[o, me] = own[o, me]
-    for o in range(m):
-        rest = arr.at[o, pl.ds(0, n - 1)]
-        pltpu.make_async_copy(rest, rest, arr_recv.at[o]).wait()
     _, _, other_score = score_of(gathered(arr))
-    asked_image = lists_in[:, 0, :][:, 0:1] // share
+    other_score = jnp.where(lax.broadcasted_iota(i32, (n, 1), 0) == me, score, other_score)
+    asked_image = lists[:, 0, :][:, 0:1] // share
+    first = column((pairs[0:1] % img_dev).astype(f32), n).astype(i32)
     for i in range(img_dev):
         scores[i] = jnp.sum(jnp.where(first == i, score, 0.0)) + jnp.sum(
             jnp.where(asked_image == i, other_score, 0.0)
         )
-
-    def drain(ref, sem):
-        pltpu.make_async_copy(ref, ref, sem).wait()
-
-    drain(whole.at[pl.ds(0, 2)], ag_send)
-    drain(whole.at[0], fw_send)
-    drain(lists_out.at[pl.ds(0, n - 1)], list_send)
-    drain(cands_out.at[pl.ds(0, n - 1)], cand_send)
-    drain(own.at[pl.ds(0, m - 1)], own_send)
-    drain(arr.at[:, pl.ds(0, n - 1)], arr_send)
 
 
 def on_device(n, m, descriptors, cell_counts, pair_images, query_cells, cand_cells, cand_counts):
@@ -276,14 +285,13 @@
     operands = (
         descriptors, cell_counts, pair_images.T, query_cells, cand_cells, cand_counts.T,
     )
-    return pl.pallas_call(
+    hbm = pl.BlockSpec(memory_space=pltpu.HBM)
+    partial = jax.ShapeDtypeStruct((m, n, 2, qd), f32)
+    own, arr, lists = pl.pallas_call(
         functools.partial(kernel, n, m),
-        out_shape=(
-            jax.ShapeDtypeStruct((n, 2, qd), f32),
-            jax.ShapeDtypeStruct((img_dev,), f32),
-        ),
-        in_specs=[pl.BlockSpec(memory_space=pltpu.HBM)] * 6,
-        out_specs=(vmem, pl.BlockSpec(memory_space=pltpu.SMEM)),
+        out_shape=(partial, partial, jax.ShapeDtypeStruct((n, 1, DESC), i32)),
+        in_specs=[hbm] * 6,
+        out_specs=(hbm,) * 3,
         scratch_shapes=[
             *(pltpu.VMEM(x.shape, x.dtype) for x in operands),
             dma((len(operands),)),
@@ -295,8 +303,7 @@
             pltpu.VMEM((n, qd, 3 * DESC), bf16),
             pltpu.VMEM((n, 8, qd), f32),
             pltpu.VMEM((n, 2, qd), f32),
-            pltpu.VMEM((m, n, 2, qd), f32),
-            pltpu.VMEM((m, n, 2, qd), f32),
+            dma((2,)),
             dma, dma((2, img_dev)), dma, dma((img_dev,)),
             dma, dma((n,)), dma, dma((n,)),
             dma, dma((m,)), dma, dma((m,)),
@@ -305,6 +312,15 @@
             collective_id=0, has_side_effects=True
         ),
     )(*operands)
+    return pl.pallas_call(
+        functools.partial(finish, n, m, img_dev, share),
+        out_shape=(
+            jax.ShapeDtypeStruct((n, 2, qd), f32),
+            jax.ShapeDtypeStruct((img_dev,), f32),
+        ),
+        in_specs=[vmem] * 4,
+        out_specs=(vmem, pl.BlockSpec(memory_space=pltpu.SMEM)),
+    )(own, arr, lists, pair_images.T)
 
 
 def solution(mesh):

time: 25.3 us -> 24.3 us (0.960)
  local copies, waits for them, and re-layouts: 1.81 us -> 0 us
  Pallas kernels: 22.6 us -> 23.5 us
    unnamed x4 -> x0, local copies, waits for them, and re-layouts: 1.81 us -> none
    pallas_call x1 -> x2, Pallas kernels: 22.6 us -> 23.5 us  [the longest x1 21.9 us: on_device(): pl.pallas_call(functools.partial(kernel, n, m), out_shape=(partial, parti...]
where the time goes in v4:
time: 24.3 us; the launch traced here: 24.1 us
  Pallas kernels  23.5 us (97%)
  between operations  0.64 us (3%)
    pallas_call x1, Pallas kernels, on_device(): pl.pallas_call(functools.partial(kernel, n, m), out_shape=(partial, parti...  21.9 us
    pallas_call x1, Pallas kernels, on_device(): pl.pallas_call(functools.partial(finish, n, m, img_dev, share), out_shape...  1.56 us

profile of v4, /device:TPU:0, one launch (start us, length us, event | category | flops | bytes accessed | tf_op | source)
XLA Modules:
  0.0 24.1 jit_solution(8766476803317116653)
XLA Ops:
  0.6 21.9 %shard_map.77 = (f32[4,8,2,128]{3,2,1,0:T(2,128)}, f32[4,8,2,128]{3,2,1,0:T(2,128)}, s32[8,1,128]{2,1,0:T(1,128)}) custom-call(bf16[2,64,1024]{2,1,0:T(8,128)(2,1)} %desc_hbm.1, s32[2,64]{1,0:T(2,128)} %counts_hbm.1, s32[2,8]{1,0:T(2,128)} %bitcast.2, s32[8,16]{1,0:T(8,128)} %qcells_hbm.1, s32[8,1,16]{2,1,0:T(1,128)} %ccells_hbm.1, s32[1,8]{1,0:T(1,128)} %bitcast.4), custom_call_target="tpu_custom_call" | custom-call | tf_op jit(solution)/shard_map/pallas_call | solution.py:290
  22.6 1.6 %shard_map.78 = (f32[8,2,128]{2,1,0:T(2,128)}, f32[2]{0:T(128)}) custom-call(f32[4,8,2,128]{3,2,1,0:T(2,128)} %get-tuple-element.5.own, f32[4,8,2,128]{3,2,1,0:T(2,128)} %get-tuple-element.6.arr, s32[8,1,128]{2,1,0:T(1,128)} %get-tuple-element.7.lists, s32[2,8]{1,0:T(2,128)} %bitcast.3), custom_call_target="tpu_custom_call" | custom-call | tf_op jit(solution)/shard_map/pallas_call | solution.py:315

commit v5 on v4

--- a/solution.py
+++ b/solution.py
@@ -139,7 +139,7 @@
         remote(shard(r, i), shard(r, i), ag_send, ag_recv.at[1, i], me, mate).start()
 
     group = n // 2
-    for g in range(0, n, group):
+    for g in (group, 0):
         picks = []
         for t in range(g, g + group):
             k = partner(me, t, n)
@@ -215,13 +215,13 @@
             [jnp.where(live, best, dead_mark), jnp.where(live, runner, dead_mark)], axis=0
         )
         part_out[j] = two
-        for d in range(1, m):
-            to_rep = partner(r, d, m)
-            remote(part_out.at[j], own.at[r, j], own_send, own_recv.at[r], me, to_rep).start()
         if not (isinstance(t, int) and t == 0):
             for d in range(m):
                 to_rep = partner(r, d, m)
                 remote(part_out.at[j], arr.at[r, me], arr_send, arr_recv.at[r], j, to_rep).start()
+        for d in range(1, m):
+            to_rep = partner(r, d, m)
+            remote(part_out.at[j], own.at[r, j], own_send, own_recv.at[r], me, to_rep).start()
 
     one_pair(0)
     repeat(1, n, one_pair)

time: 24.3 us -> 23.9 us (0.984)
  Pallas kernels: 23.5 us -> 23.1 us
    pallas_call x1, Pallas kernels: 21.9 us -> 21.5 us  [on_device(): pl.pallas_call(functools.partial(kernel, n, m), out_shape=(partial, parti...]
where the time goes in v5:
time: 23.9 us; the launch traced here: 23.7 us
  Pallas kernels  23.1 us (97%)
  between operations  0.64 us (3%)
    pallas_call x1, Pallas kernels, on_device(): pl.pallas_call(functools.partial(kernel, n, m), out_shape=(partial, parti...  21.5 us
    pallas_call x1, Pallas kernels, on_device(): pl.pallas_call(functools.partial(finish, n, m, img_dev, share), out_shape...  1.56 us

profile of v5, /device:TPU:0, one launch (start us, length us, event | category | flops | bytes accessed | tf_op | source)
XLA Modules:
  0.0 23.7 jit_solution(12341213838042448681)
XLA Ops:
  0.6 21.5 %shard_map.77 = (f32[4,8,2,128]{3,2,1,0:T(2,128)}, f32[4,8,2,128]{3,2,1,0:T(2,128)}, s32[8,1,128]{2,1,0:T(1,128)}) custom-call(bf16[2,64,1024]{2,1,0:T(8,128)(2,1)} %desc_hbm.1, s32[2,64]{1,0:T(2,128)} %counts_hbm.1, s32[2,8]{1,0:T(2,128)} %bitcast.2, s32[8,16]{1,0:T(8,128)} %qcells_hbm.1, s32[8,1,16]{2,1,0:T(1,128)} %ccells_hbm.1, s32[1,8]{1,0:T(1,128)} %bitcast.4), custom_call_target="tpu_custom_call" | custom-call | tf_op jit(solution)/shard_map/pallas_call | solution.py:290
  22.1 1.6 %shard_map.78 = (f32[8,2,128]{2,1,0:T(2,128)}, f32[2]{0:T(128)}) custom-call(f32[4,8,2,128]{3,2,1,0:T(2,128)} %get-tuple-element.5.own, f32[4,8,2,128]{3,2,1,0:T(2,128)} %get-tuple-element.6.arr, s32[8,1,128]{2,1,0:T(1,128)} %get-tuple-element.7.lists, s32[2,8]{1,0:T(2,128)} %bitcast.3), custom_call_target="tpu_custom_call" | custom-call | tf_op jit(solution)/shard_map/pallas_call | solution.py:315
